TPU v7x, 32 devices: a whole 2x2x4 slice. The times are simulated.
32 devices in a mesh: dp: 16 (over z, y, x), mp: 2 (over core).
Axes of the slice: x: 2, y: 2, z: 4, core: 2. Of those that a mesh axis runs over, the one named last changes fastest.
Arguments:
- tokens: bfloat16 [32768, 768], P('dp'), may hold values from -6 to 6
- segments: int32 [32768], P('dp'), may hold values from 0 to 32, as said below
- sentence_dest: int32 [2048, 2], P('dp'), may hold values from 0 to 15, as said below
- pair_source: int32 [2048, 2], P('dp'), may hold values from 0 to 15, as said below
- labels: int32 [1024], P('dp'), may hold values from 0 to 5
- params: float32 [2, 3541248], P('mp', 'dp'), as said below
- first: float32 [2, 3541248], P('mp', 'dp')
- second: float32 [2, 3541248], P('mp', 'dp'), as said below
- shared: float32 [6, 768], replicated, as said below
- shared_first: float32 [6, 768], replicated
- shared_second: float32 [6, 768], replicated, as said below
Outputs:
- encoded: bfloat16 [32768, 768], P('dp')
- input_grad: float32 [32768, 768], P('dp')
- grad_norm: float32 [1], replicated
- params_new: float32 [2, 3541248], P('mp', 'dp')
- first_new: float32 [2, 3541248], P('mp', 'dp')
- second_new: float32 [2, 3541248], P('mp', 'dp')
- params_low: bfloat16 [2, 3541248], P('mp', 'dp')
- shared_new: float32 [6, 768], replicated
- shared_first_new: float32 [6, 768], replicated
- shared_second_new: float32 [6, 768], replicated
- params_grad: float32 [2, 3541248], P('mp', 'dp')
- shared_grad: float32 [6, 768], replicated
Inputs may be any that keep to these rules, and one draw needn't show every extreme that they name: `segments`: within each row of 512 positions ids never fall; each id 0 to 31 covers 1 to 16 positions and slot 0 exactly 16; id 32 marks the padding at a row's end. `sentence_dest`: column 0 is the scoring device, column 1 the place 0 to 7 among the sentences that this device sends there; each device sends exactly 8 or none of its sentences to each device, and each (device, place) occurs once per sender. `pair_source`: column 0 is the sending device, column 1 the place; each names a sentence whose sentence_dest points to this device and place, every sentence exactly once; items 2j and 2j+1 form pair j. `params`: laid out as the steps say. `second`: Positive. `shared`: Rows: first gain, first bias, second gain, second bias, attention output bias, feed-forward output bias. `shared_second`: Positive.
All inputs are finite; a program needn't handle non-finite values.
Results may differ from a plain program's by a relative error of at most 0.018.
Values may be sent and summed in bfloat16 or wider, within the bound.
A program may use at most 256 MiB of HBM per device.

v0:
```python
from functools import partial
import math
import jax
import jax.numpy as jnp
from jax import lax
from jax.sharding import PartitionSpec as P

HEAD_DIM = 64
FF = 3072
ROW = 512
SEG = 32
RPM = 2
MB = 2
LOSS_SCALE = 1024.0
CLIP_NORM = 0.5
LEARN_RATE = 0.1
SHARED_RATE = 0.5
BETA_ONE = 0.9
BETA_TWO = 0.999
ADAM_EPS = 1e-08
DECAY = 0.01
NORM_EPS = 1e-12
STEP_COUNT = 10.0
TOP_PRECISION = lax.Precision.HIGHEST


def normalize(values_in, scale_vec, shift_vec):
    center = jnp.mean(values_in, -1, keepdims=True)
    centered = values_in - center
    spread = jnp.mean(centered * centered, -1, keepdims=True)
    return centered * lax.rsqrt(spread + NORM_EPS) * scale_vec + shift_vec


def unpack(packed, features, head_cols, ffn_cols):
    pieces = []
    offset = 0
    for height, extent in (
        (features, 3 * head_cols),
        (head_cols, features),
        (features, ffn_cols),
        (ffn_cols, features),
    ):
        pieces.append(packed[offset : offset + height * extent].reshape(height, extent))
        offset = offset + height * extent
    for extent in (head_cols, head_cols, ffn_cols):
        pieces.append(packed[offset : offset + extent])
        offset = offset + extent
    return pieces


def pair_loss(pair_items, labels):
    first_vec = pair_items[..., 0::2, :]
    second_vec = pair_items[..., 1::2, :]
    inner_prod = jnp.sum(first_vec * second_vec, -1)
    cosine = (
        inner_prod
        * lax.rsqrt(jnp.sum(first_vec * first_vec, -1) + 1e-06)
        * lax.rsqrt(jnp.sum(second_vec * second_vec, -1) + 1e-06)
    )
    error_term = cosine - labels.astype(jnp.float32) / 5.0
    return LOSS_SCALE * jnp.sum(error_term * error_term)


def adamw(weight, moment_one, moment_two, gradient, factor, step_count, rate):
    clipped = gradient * factor
    first_new = BETA_ONE * moment_one + (1.0 - BETA_ONE) * clipped
    second_new = BETA_TWO * moment_two + (1.0 - BETA_TWO) * clipped * clipped
    first_hat = first_new / (1.0 - BETA_ONE**step_count)
    second_hat = second_new / (1.0 - BETA_TWO**step_count)
    weight_new = weight - rate * (first_hat / (jnp.sqrt(second_hat) + ADAM_EPS) + DECAY * weight)
    return (weight_new, first_new, second_new)


def per_device(
    tokens,
    segments,
    sentence_dest,
    pair_source,
    labels,
    params,
    first,
    second,
    shared,
    shared_first,
    shared_second,
):
    features = tokens.shape[1]
    head_cols = features // lax.axis_size("mp")
    ffn_cols = FF // lax.axis_size("mp")
    heads_dev = head_cols // HEAD_DIM
    dp_count = lax.axis_size("dp")
    sent_slots = MB * RPM * SEG
    slot_capacity = max(2, sent_slots // dp_count)
    score_scale = HEAD_DIM ** (-0.5)
    flat_rows = RPM * ROW
    params_total = lax.axis_size("mp") * params.shape[1] * dp_count + 6 * features
    low_shard = params.astype(jnp.bfloat16)

    def weights_now():
        return unpack(
            lax.all_gather(low_shard, "dp", axis=1, tiled=True)[0], features, head_cols, ffn_cols
        )

    slot_ids = jnp.arange(SEG, dtype=jnp.int32)

    def pooling_matrix(block_segments):
        onehot = (block_segments[:, None, :] == slot_ids[None, :, None]).astype(jnp.float32)
        return onehot / jnp.sum(onehot, 2, keepdims=True)

    def masked_scores(queries, keys_low, block_segments):
        same_doc = (block_segments[:, :, None] == block_segments[:, None, :])[:, None]
        scores = (
            jnp.einsum("rqhd,rkhd->rhqk", queries, keys_low, preferred_element_type=jnp.float32)
            * score_scale
        )
        return jnp.where(same_doc, scores, -1e30)

    def forward_step(carried, inputs):
        tokens_block, block_segments = inputs
        w_qkv, w_attn, w_in, w_out, b_query, b_value, b_in = weights_now()
        tokens_flat = tokens_block.reshape(flat_rows, features)
        projected = jnp.dot(tokens_flat, w_qkv, preferred_element_type=jnp.float32)
        queries = (
            (projected[:, :head_cols] + b_query)
            .astype(jnp.bfloat16)
            .reshape(RPM, ROW, heads_dev, HEAD_DIM)
        )
        keys_low = (
            projected[:, head_cols : 2 * head_cols]
            .astype(jnp.bfloat16)
            .reshape(RPM, ROW, heads_dev, HEAD_DIM)
        )
        values_low = (
            (projected[:, 2 * head_cols :] + b_value)
            .astype(jnp.bfloat16)
            .reshape(RPM, ROW, heads_dev, HEAD_DIM)
        )
        scores = masked_scores(queries, keys_low, block_segments)
        row_max = jnp.max(scores, -1, keepdims=True)
        exponent = jnp.exp(scores - row_max)
        row_total = jnp.sum(exponent, -1, keepdims=True)
        attn_probs = (exponent / row_total).astype(jnp.bfloat16)
        log_total = row_max + jnp.log(row_total)
        mixed_heads = jnp.einsum(
            "rhqk,rkhd->rqhd", attn_probs, values_low, preferred_element_type=jnp.float32
        )
        mixed_heads = mixed_heads.reshape(flat_rows, head_cols).astype(jnp.bfloat16)
        attn_term = jnp.dot(mixed_heads, w_attn, preferred_element_type=jnp.float32)
        attn_out = lax.psum(attn_term.astype(jnp.bfloat16), "mp").astype(jnp.float32) + shared[4]
        resid_one = tokens_flat.astype(jnp.float32) + attn_out
        hidden = normalize(resid_one, shared[0], shared[1])
        up_proj = (
            jnp.dot(hidden.astype(jnp.bfloat16), w_in, preferred_element_type=jnp.float32) + b_in
        )
        activated = jax.nn.gelu(up_proj, approximate=False).astype(jnp.bfloat16)
        ffn_term = jnp.dot(activated, w_out, preferred_element_type=jnp.float32)
        ffn_out = lax.psum(ffn_term.astype(jnp.bfloat16), "mp").astype(jnp.float32) + shared[5]
        resid_two = hidden + ffn_out
        encoded_flat = normalize(resid_two, shared[2], shared[3])
        block_encodings = encoded_flat.reshape(RPM, ROW, features)
        pooled = jnp.einsum(
            "kvf,kfo->kvo", pooling_matrix(block_segments), block_encodings, precision=TOP_PRECISION
        ).astype(jnp.bfloat16)
        saved_state = (
            queries,
            keys_low,
            values_low,
            log_total,
            mixed_heads,
            resid_one,
            up_proj,
            activated,
            resid_two,
        )
        return (carried, (block_encodings.astype(jnp.bfloat16), pooled, saved_state))

    token_blocks = tokens.reshape(MB, RPM, ROW, features)
    segment_blocks = segments.reshape(MB, RPM, ROW)
    ignored, (encoded, pooled_all, saved_all) = lax.scan(
        forward_step, jnp.zeros((), jnp.float32), (token_blocks, segment_blocks)
    )
    pooled_flat = pooled_all.reshape(sent_slots, features)
    code_ids = jnp.arange(dp_count * slot_capacity, dtype=jnp.int32)
    send_code = sentence_dest[:, 0] * slot_capacity + sentence_dest[:, 1]
    send_map = (code_ids[:, None] == send_code[None, :]).astype(jnp.bfloat16)
    outgoing = jnp.dot(send_map, pooled_flat, preferred_element_type=jnp.float32).astype(
        jnp.bfloat16
    )
    outgoing = outgoing.reshape(dp_count, slot_capacity, features)
    incoming = lax.all_to_all(outgoing, "dp", split_axis=0, concat_axis=0, tiled=True).reshape(
        dp_count * slot_capacity, features
    )
    take_code = pair_source[:, 0] * slot_capacity + pair_source[:, 1]
    take_map = (take_code[:, None] == code_ids[None, :]).astype(jnp.bfloat16)
    pair_items = jnp.dot(take_map, incoming, preferred_element_type=jnp.float32)
    item_grad = jax.grad(pair_loss)(pair_items, labels).astype(jnp.bfloat16)
    returning = jnp.dot(take_map.T, item_grad, preferred_element_type=jnp.float32).astype(
        jnp.bfloat16
    )
    returning = returning.reshape(dp_count, slot_capacity, features)
    arrived = lax.all_to_all(returning, "dp", split_axis=0, concat_axis=0, tiled=True).reshape(
        dp_count * slot_capacity, features
    )
    pooled_grad = jnp.dot(send_map.T, arrived, preferred_element_type=jnp.float32).reshape(
        MB, RPM, SEG, features
    )

    def backward_step(carried, inputs):
        shared_acc, flat_acc = carried
        tokens_block, block_segments, sentence_gradient, saved_state = inputs
        (
            queries,
            keys_low,
            values_low,
            log_total,
            mixed_heads,
            resid_one,
            up_proj,
            activated,
            resid_two,
        ) = saved_state
        w_qkv, w_attn, w_in, w_out, b_query, b_value, b_in = weights_now()
        tokens_flat = tokens_block.reshape(flat_rows, features)
        encoded_grad = jnp.einsum(
            "jix,jip->jxp",
            pooling_matrix(block_segments),
            sentence_gradient,
            precision=TOP_PRECISION,
        ).reshape(flat_rows, features)
        ignored_two, norm_two_back = jax.vjp(normalize, resid_two, shared[2], shared[3])
        resid_two_grad, scale_two, shift_two = norm_two_back(encoded_grad)
        ffn_grad = resid_two_grad.astype(jnp.bfloat16)
        ignored_act, gelu_back = jax.vjp(partial(jax.nn.gelu, approximate=False), up_proj)
        act_grad = jnp.dot(ffn_grad, w_out.T, preferred_element_type=jnp.float32)
        up_grad = gelu_back(act_grad)[0].astype(jnp.bfloat16)
        hidden, norm_one_back = jax.vjp(normalize, resid_one, shared[0], shared[1])
        w_out_grad = jnp.dot(activated.T, ffn_grad, preferred_element_type=jnp.float32)
        w_in_grad = jnp.dot(
            hidden.astype(jnp.bfloat16).T, up_grad, preferred_element_type=jnp.float32
        )
        hidden_term = jnp.dot(up_grad, w_in.T, preferred_element_type=jnp.float32)
        hidden_grad = resid_two_grad + lax.psum(hidden_term.astype(jnp.bfloat16), "mp").astype(
            jnp.float32
        )
        resid_one_grad, scale_one, shift_one = norm_one_back(hidden_grad)
        attn_grad = resid_one_grad.astype(jnp.bfloat16)
        w_attn_grad = jnp.dot(mixed_heads.T, attn_grad, preferred_element_type=jnp.float32)
        mixed_grad = jnp.dot(attn_grad, w_attn.T, preferred_element_type=jnp.float32)
        mixed_grad = mixed_grad.astype(jnp.bfloat16).reshape(RPM, ROW, heads_dev, HEAD_DIM)
        attn_probs = jnp.exp(masked_scores(queries, keys_low, block_segments) - log_total)
        value_grad = jnp.einsum(
            "rhqk,rqhd->rkhd",
            attn_probs.astype(jnp.bfloat16),
            mixed_grad,
            preferred_element_type=jnp.float32,
        )
        prob_grad = jnp.einsum(
            "rqhd,rkhd->rhqk", mixed_grad, values_low, preferred_element_type=jnp.float32
        )
        row_inner = jnp.sum(prob_grad * attn_probs, -1, keepdims=True)
        score_grad = (attn_probs * (prob_grad - row_inner)).astype(jnp.bfloat16)
        query_grad = (
            jnp.einsum("rhqk,rkhd->rqhd", score_grad, keys_low, preferred_element_type=jnp.float32)
            * score_scale
        )
        key_grad = (
            jnp.einsum("rhqk,rqhd->rkhd", score_grad, queries, preferred_element_type=jnp.float32)
            * score_scale
        )
        query_key_value_gradient = jnp.concatenate(
            [
                query_grad.reshape(flat_rows, head_cols),
                key_grad.reshape(flat_rows, head_cols),
                value_grad.reshape(flat_rows, head_cols),
            ],
            1,
        ).astype(jnp.bfloat16)
        w_qkv_grad = jnp.dot(
            tokens_flat.T, query_key_value_gradient, preferred_element_type=jnp.float32
        )
        input_term = jnp.dot(query_key_value_gradient, w_qkv.T, preferred_element_type=jnp.float32)
        input_grad = resid_one_grad + lax.psum(input_term.astype(jnp.bfloat16), "mp").astype(
            jnp.float32
        )
        column_sums = jnp.sum(query_key_value_gradient.astype(jnp.float32), 0)
        grad_flat = jnp.concatenate(
            [
                w_qkv_grad.reshape(-1),
                w_attn_grad.reshape(-1),
                w_in_grad.reshape(-1),
                w_out_grad.reshape(-1),
                column_sums[:head_cols],
                column_sums[2 * head_cols :],
                jnp.sum(up_grad.astype(jnp.float32), 0),
            ]
        )[None]
        shared_step = jnp.stack(
            [
                scale_one,
                shift_one,
                scale_two,
                shift_two,
                jnp.sum(attn_grad.astype(jnp.float32), 0),
                jnp.sum(ffn_grad.astype(jnp.float32), 0),
            ]
        )
        flat_acc = flat_acc + lax.psum_scatter(grad_flat, "dp", scatter_dimension=1, tiled=True)
        return ((shared_acc + shared_step, flat_acc), input_grad)

    flat_start = jnp.zeros((1, params.shape[1]), jnp.float32)
    (shared_acc, flat_acc), input_grads = lax.scan(
        backward_step,
        (jnp.zeros_like(shared), flat_start),
        (token_blocks, segment_blocks, pooled_grad, saved_all),
    )
    flat_grad = flat_acc
    flat_grad = flat_grad / LOSS_SCALE
    local_squares = jnp.sum(flat_grad * flat_grad)
    shared_total = lax.psum(shared_acc, "dp")
    total_squares = lax.psum(local_squares, ("dp", "mp"))
    shared_grad = shared_total / LOSS_SCALE
    norm_value = jnp.sqrt(total_squares + jnp.sum(shared_grad * shared_grad))
    factor = jnp.minimum(1.0, CLIP_NORM / norm_value)
    step_count = STEP_COUNT
    params_new, first_new, second_new = adamw(
        params, first, second, flat_grad, factor, step_count, LEARN_RATE
    )
    shared_new, shared_first_new, shared_second_new = adamw(
        shared, shared_first, shared_second, shared_grad, factor, step_count, SHARED_RATE
    )
    grad_unit = math.sqrt(params_total) / CLIP_NORM
    params_grad = flat_grad * factor * grad_unit
    shared_grad_out = shared_grad * factor * grad_unit
    return (
        encoded.reshape(MB * RPM * ROW, features),
        input_grads.reshape(MB * RPM * ROW, features),
        norm_value.reshape(1),
        params_new,
        first_new,
        second_new,
        params_new.astype(jnp.bfloat16),
        shared_new,
        shared_first_new,
        shared_second_new,
        params_grad,
        shared_grad_out,
    )


def solution(mesh):
    in_specs = (
        P("dp", None),
        P("dp"),
        P("dp", None),
        P("dp", None),
        P("dp"),
        P("mp", "dp"),
        P("mp", "dp"),
        P("mp", "dp"),
        P(),
        P(),
        P(),
    )
    out_specs = (
        P("dp", None),
        P("dp", None),
        P(),
        P("mp", "dp"),
        P("mp", "dp"),
        P("mp", "dp"),
        P("mp", "dp"),
        P(),
        P(),
        P(),
        P("mp", "dp"),
        P(),
    )
    return jax.shard_map(
        per_device, mesh=mesh, in_specs=in_specs, out_specs=out_specs, check_vma=False
    )
```

profile of v0, /device:TPU:0, one launch (start us, length us, event | category | flops | bytes accessed | tf_op | source)
XLA Modules:
  0.0 3310.9 jit_solution(3628532116276965584)
XLA Ops:
  18.3 1072.0 %while.46 = (s32[]{:T(128)}, bf16[2,2,512,768]{3,2,1,0:T(8,128)(2,1)}, bf16[2,2,32,768]{3,2,1,0:T(8,128)(2,1)S(1)}, bf16[2,2,512,6,64]{2,1,4,3,0:T(2,128)(2,1)},...) while((s32[]{:T(128)}, ...), condition=%wide.region_10.11_spmd.clone, body=%wide.region_0.10_spmd.clone.sunk | while | flops 8542994944 | bytes 398459968 | solution.py:179
  43.5 228.5 %all-reduce.21.cloned.1.call-done = bf16[3541248]{0:T(1024)(128)(2,1)} async-done(((bf16[3541248]{0:T(1024)(128)(2,1)}), bf16[3541248]{0:T(1024)(128)(2,1)}) %all-reduce.21.cloned.1.call-update) | async-done | bytes 7082512 | tf_op jit(solution)/shard_map/while
  272.0 69.0 %reshape.574 = bf16[1,3541248]{1,0:T(2,128)(2,1)S(1)} reshape(bf16[3541248]{0:T(1024)(128)(2,1)} %all-reduce.21.cloned.1.call-done) | data formatting | bytes 14164992 | tf_op jit(solution)/shard_map/while
  351.7 35.6 %slice_reduce_fusion.27 = bf16[884736]{0:T(1024)(128)(2,1)} fusion(bf16[1,3541248]{1,0:T(2,128)(2,1)S(1)} %reshape.574), kind=kLoop, calls=%fused_computation.30.clone.1 | loop fusion | bytes 3538944 | tf_op jit(solution)/shard_map/while/body/eval_jaxpr/slice | solution.py:43
  429.7 53.2 %slice_reduce_fusion.26 = (bf16[1179648]{0:T(1024)(128)(2,1)}, bf16[1179648]{0:T(1024)(128)(2,1)}) fusion(bf16[1,3541248]{1,0:T(2,128)(2,1)} %copy-done.2), kind=kLoop, calls=%fused_computation.28.clone.1 | loop fusion | bytes 9437184 | tf_op jit(solution)/shard_map/while/body/eval_jaxpr/slice | solution.py:43
  503.0 17.9 bitcast_dynamic-update-slice_fusion.12
  579.2 227.0 %all-reduce.21.cloned.1.call-done = bf16[3541248]{0:T(1024)(128)(2,1)} async-done(((bf16[3541248]{0:T(1024)(128)(2,1)}), bf16[3541248]{0:T(1024)(128)(2,1)}) %all-reduce.21.cloned.1.call-update) | async-done | bytes 7082512 | tf_op jit(solution)/shard_map/while
  806.2 68.9 %reshape.574 = bf16[1,3541248]{1,0:T(2,128)(2,1)S(1)} reshape(bf16[3541248]{0:T(1024)(128)(2,1)} %all-reduce.21.cloned.1.call-done) | data formatting | bytes 14164992 | tf_op jit(solution)/shard_map/while
  885.8 35.6 %slice_reduce_fusion.27 = bf16[884736]{0:T(1024)(128)(2,1)} fusion(bf16[1,3541248]{1,0:T(2,128)(2,1)S(1)} %reshape.574), kind=kLoop, calls=%fused_computation.30.clone.1 | loop fusion | bytes 3538944 | tf_op jit(solution)/shard_map/while/body/eval_jaxpr/slice | solution.py:43
  963.8 53.2 %slice_reduce_fusion.26 = (bf16[1179648]{0:T(1024)(128)(2,1)}, bf16[1179648]{0:T(1024)(128)(2,1)}) fusion(bf16[1,3541248]{1,0:T(2,128)(2,1)} %copy-done.2), kind=kLoop, calls=%fused_computation.28.clone.1 | loop fusion | bytes 9437184 | tf_op jit(solution)/shard_map/while/body/eval_jaxpr/slice | solution.py:43
  1037.1 17.9 bitcast_dynamic-update-slice_fusion.12
  1124.7 2047.9 %while.47 = (s32[]{:T(128)}, f32[6,768]{1,0:T(8,128)}, f32[1,221328]{1,0:T(1,128)}, f32[2,1024,768]{2,1,0:T(8,128)}, f32[2,1024,768]{2,1,0:T(8,128)}, /*index=5*...) while((s32[]{:T(128)}, f32[6,768]{1,0:T(8,128)}, ...), condition=%wide.region_36.37_spmd.clone, body=%wide.region_14.36_spmd.clone.sunk | while | flops 17043947520 | bytes 761370240 | solution.py:311
  1192.5 181.0 %all-reduce.27.cloned.1.call-done = bf16[3541248]{0:T(1024)(128)(2,1)} async-done(((bf16[3541248]{0:T(1024)(128)(2,1)}), bf16[3541248]{0:T(1024)(128)(2,1)}) %all-reduce.27.cloned.1.call-update) | async-done | bytes 7082512 | tf_op jit(solution)/shard_map/while
  1373.5 68.6 %reshape.582 = bf16[1,3541248]{1,0:T(2,128)(2,1)} reshape(bf16[3541248]{0:T(1024)(128)(2,1)} %all-reduce.27.cloned.1.call-done) | data formatting | bytes 14164992 | tf_op jit(solution)/shard_map/while
  1442.1 53.6 %slice_reduce_fusion.30 = (bf16[1179648]{0:T(1024)(128)(2,1)}, bf16[1179648]{0:T(1024)(128)(2,1)}) fusion(bf16[1,3541248]{1,0:T(2,128)(2,1)} %reshape.582), kind=kLoop, calls=%fused_computation.138.clone.1 | loop fusion | bytes 9437184 | tf_op jit(solution)/shard_map/while/body/eval_jaxpr/slice | solution.py:43
  1506.5 19.6 convert_reduce_fusion.15
  1531.6 11.8 slice_reduce_fusion.31
  1545.7 36.6 %slice_reduce_fusion.32 = bf16[884736]{0:T(1024)(128)(2,1)} fusion(bf16[1,3541248]{1,0:T(2,128)(2,1)} %reshape.582), kind=kLoop, calls=%fused_computation.141.clone.1 | loop fusion | bytes 3538944 | tf_op jit(solution)/shard_map/while/body/eval_jaxpr/slice | solution.py:43
  1626.1 11.4 multiply_reduce_fusion.27
  1691.6 54.1 %broadcast_in_dim.266 = f32[1,3541248]{1,0:T(1,128)} reshape(f32[3541248]{0:T(1024)} %constant_dynamic-update-slice_fusion.42) | data formatting | bytes 28329984 | tf_op jit(solution)/shard_map/while/body/eval_jaxpr/broadcast_in_dim | solution.py:286
  1750.8 391.5 %all-reduce.31.cloned.1.call-done = f32[1,3541248]{1,0:T(1,128)} async-done(((f32[1,3541248]{1,0:T(1,128)}), f32[1,3541248]{1,0:T(1,128)}) %all-reduce.31.cloned.1.call-update) | async-done | bytes 14165008 | tf_op jit(solution)/shard_map/while
  2213.9 182.4 %all-reduce.27.cloned.1.call-done = bf16[3541248]{0:T(1024)(128)(2,1)} async-done(((bf16[3541248]{0:T(1024)(128)(2,1)}), bf16[3541248]{0:T(1024)(128)(2,1)}) %all-reduce.27.cloned.1.call-update) | async-done | bytes 7082512 | tf_op jit(solution)/shard_map/while
  2396.3 68.6 %reshape.582 = bf16[1,3541248]{1,0:T(2,128)(2,1)} reshape(bf16[3541248]{0:T(1024)(128)(2,1)} %all-reduce.27.cloned.1.call-done) | data formatting | bytes 14164992 | tf_op jit(solution)/shard_map/while
  2464.9 53.3 %slice_reduce_fusion.30 = (bf16[1179648]{0:T(1024)(128)(2,1)}, bf16[1179648]{0:T(1024)(128)(2,1)}) fusion(bf16[1,3541248]{1,0:T(2,128)(2,1)} %reshape.582), kind=kLoop, calls=%fused_computation.138.clone.1 | loop fusion | bytes 9437184 | tf_op jit(solution)/shard_map/while/body/eval_jaxpr/slice | solution.py:43
  2529.1 19.6 convert_reduce_fusion.15
  2554.2 11.9 slice_reduce_fusion.31
  2568.4 36.6 %slice_reduce_fusion.32 = bf16[884736]{0:T(1024)(128)(2,1)} fusion(bf16[1,3541248]{1,0:T(2,128)(2,1)} %reshape.582), kind=kLoop, calls=%fused_computation.141.clone.1 | loop fusion | bytes 3538944 | tf_op jit(solution)/shard_map/while/body/eval_jaxpr/slice | solution.py:43
  2648.9 11.4 multiply_reduce_fusion.27
  2714.4 54.1 %broadcast_in_dim.266 = f32[1,3541248]{1,0:T(1,128)} reshape(f32[3541248]{0:T(1024)} %constant_dynamic-update-slice_fusion.42) | data formatting | bytes 28329984 | tf_op jit(solution)/shard_map/while/body/eval_jaxpr/broadcast_in_dim | solution.py:286
  2773.6 391.5 %all-reduce.31.cloned.1.call-done = f32[1,3541248]{1,0:T(1,128)} async-done(((f32[1,3541248]{1,0:T(1,128)}), f32[1,3541248]{1,0:T(1,128)}) %all-reduce.31.cloned.1.call-update) | async-done | bytes 14165008 | tf_op jit(solution)/shard_map/while
  3176.1 39.5 %psum.42 = f32[]{:T(128)} all-reduce(f32[]{:T(128)} %multiply_reduce_fusion.9), channel_id=1, replica_groups=mesh['dp'=16,'mp'=2] {'dp','mp'}, use_global_device_ids=true, to_apply=%region_38.39 | all-reduce | flops 1 | bytes 8 | tf_op jit(solution)/shard_map/psum | solution.py:320
  3215.6 75.8 %psum.43 = f32[6,768]{1,0:T(8,128)S(1)} all-reduce(f32[6,768]{1,0:T(8,128)} %get-tuple-element.221), channel_id=1, replica_groups=mesh['dp'=16,'mp'=2] {'dp'}, use_global_device_ids=true, to_apply=%region_39.40 | all-reduce | flops 4608 | bytes 36864 | tf_op jit(solution)/shard_map/psum | solution.py:319
  (565 shorter events, 701.5 us)
Async XLA Ops:
  18.3 1072.0 %copy-start.45 = (s32[128]{0:T(128)S(1)}, s32[128]{0:T(128)}, u32[]{:S(2)}) copy-start(s32[128]{0:T(128)} %add_bitcast_fusion.1) | copy-start | bytes 1540
  18.3 1079.7 %copy-start.50 = (s32[128,2]{0,1:T(2,128)S(1)}, s32[128,2]{0,1:T(2,128)}, u32[]{:S(2)}) copy-start(s32[128,2]{0,1:T(2,128)} %param.18) | copy-start | bytes 3076
  18.3 1089.5 %copy-start.46 = (s32[64]{0:T(128)S(1)}, s32[64]{0:T(128)}, u32[]{:S(2)}) copy-start(s32[64]{0:T(128)} %param.19) | copy-start | bytes 772
  18.5 253.5 %all-reduce.21.cloned.1.call-start = ((), (), s32[]{:S(2)}) async-start(), calls=%async_computation.2 | async-start | bytes 14168064 | tf_op jit(solution)/shard_map/while
  39.9 460.0 %all-reduce.23.cloned.1.call-start = ((), (), s32[]{:S(2)}) async-start(), calls=%async_computation.3 | async-start | bytes 3145728 | tf_op jit(solution)/shard_map/while/body/eval_jaxpr/psum | solution.py:149
  429.6 114.6 %all-reduce.25.cloned.1.call-start = ((), (), s32[]{:S(2)}) async-start(), calls=%async_computation.4 | async-start | bytes 3145728 | tf_op jit(solution)/shard_map/while/body/eval_jaxpr/psum | solution.py:157
  503.0 17.9 copy-start.23
  554.2 252.0 %all-reduce.21.cloned.1.call-start = ((), (), s32[]{:S(2)}) async-start(), calls=%async_computation.2 | async-start | bytes 14168064 | tf_op jit(solution)/shard_map/while
  575.6 458.4 %all-reduce.23.cloned.1.call-start = ((), (), s32[]{:S(2)}) async-start(), calls=%async_computation.3 | async-start | bytes 3145728 | tf_op jit(solution)/shard_map/while/body/eval_jaxpr/psum | solution.py:149
  963.7 114.6 %all-reduce.25.cloned.1.call-start = ((), (), s32[]{:S(2)}) async-start(), calls=%async_computation.4 | async-start | bytes 3145728 | tf_op jit(solution)/shard_map/while/body/eval_jaxpr/psum | solution.py:157
  1091.2 15.9 all-to-all-start
  1109.0 11.6 all-to-all-start.1
  1124.7 2168.8 %copy-start.43 = (f32[6,768]{1,0:T(8,128)S(1)}, f32[6,768]{1,0:T(8,128)}, u32[]{:S(2)}) copy-start(f32[6,768]{1,0:T(8,128)} %param.24) | copy-start | bytes 55300
  1124.7 2168.8 %copy-start.44 = (f32[6,768]{1,0:T(8,128)S(1)}, f32[6,768]{1,0:T(8,128)}, u32[]{:S(2)}) copy-start(f32[6,768]{1,0:T(8,128)} %param.25) | copy-start | bytes 55300
  1124.8 24.5 copy-start.34
  1124.9 51.6 %copy-start.39 = (f32[2,2,6,512,1]{3,2,1,4,0:T(8,128)}, f32[2,2,6,512,1]{3,2,1,4,0:T(8,128)S(1)}, u32[]{:S(2)}) copy-start(f32[2,2,6,512,1]{3,2,1,4,0:T(8,128)S(1)} %get-tuple-element.975) | copy-start | bytes 147460 | tf_op jit(solution)/shard_map/while
  1124.9 248.6 %all-reduce.27.cloned.1.call-start = ((), (), s32[]{:S(2)}) async-start(), calls=%async_computation.5 | async-start | bytes 14168064 | tf_op jit(solution)/shard_map/while
  1146.2 454.4 %all-reduce.29.cloned.1.call-start = ((), (), s32[]{:S(2)}) async-start(), calls=%async_computation.6 | async-start | bytes 3145728 | tf_op jit(solution)/shard_map/while/body/eval_jaxpr/psum | solution.py:242
  1506.5 21.2 copy-start.24
  1531.5 215.7 %all-reduce.33.cloned.1.call-start = ((), (), s32[]{:S(2)}) async-start(), calls=%async_computation.8 | async-start | bytes 3145728 | tf_op jit(solution)/shard_map/while/body/eval_jaxpr/psum | solution.py:282
  1663.0 479.2 %all-reduce.31.cloned.1.call-start = ((), (), s32[]{:S(2)}) async-start(), calls=%async_computation.7 | async-start | bytes 28329984 | tf_op jit(solution)/shard_map/while
  1747.2 398.8 %copy-start.35 = (f32[6,768]{1,0:T(8,128)S(1)}, f32[6,768]{1,0:T(8,128)}, u32[]{:S(2)}) copy-start(f32[6,768]{1,0:T(8,128)} %copy-done.34) | copy-start | bytes 55300 | tf_op jit(solution)/shard_map/while
  1747.3 398.8 %copy-start.40 = (f32[2,2,6,512,1]{3,2,1,4,0:T(8,128)S(1)}, f32[2,2,6,512,1]{3,2,1,4,0:T(8,128)}, u32[]{:S(2)}) copy-start(f32[2,2,6,512,1]{3,2,1,4,0:T(8,128)} %copy-done.39) | copy-start | bytes 147460 | tf_op jit(solution)/shard_map/while
  2146.3 24.5 copy-start.34
  2146.3 51.8 %copy-start.39 = (f32[2,2,6,512,1]{3,2,1,4,0:T(8,128)}, f32[2,2,6,512,1]{3,2,1,4,0:T(8,128)S(1)}, u32[]{:S(2)}) copy-start(f32[2,2,6,512,1]{3,2,1,4,0:T(8,128)S(1)} %get-tuple-element.975) | copy-start | bytes 147460 | tf_op jit(solution)/shard_map/while
  2146.3 250.0 %all-reduce.27.cloned.1.call-start = ((), (), s32[]{:S(2)}) async-start(), calls=%async_computation.5 | async-start | bytes 14168064 | tf_op jit(solution)/shard_map/while
  2167.7 455.8 %all-reduce.29.cloned.1.call-start = ((), (), s32[]{:S(2)}) async-start(), calls=%async_computation.6 | async-start | bytes 3145728 | tf_op jit(solution)/shard_map/while/body/eval_jaxpr/psum | solution.py:242
  2529.1 21.2 copy-start.24
  2554.1 215.9 %all-reduce.33.cloned.1.call-start = ((), (), s32[]{:S(2)}) async-start(), calls=%async_computation.8 | async-start | bytes 3145728 | tf_op jit(solution)/shard_map/while/body/eval_jaxpr/psum | solution.py:282
  2685.8 479.3 %all-reduce.31.cloned.1.call-start = ((), (), s32[]{:S(2)}) async-start(), calls=%async_computation.7 | async-start | bytes 28329984 | tf_op jit(solution)/shard_map/while
  2770.1 399.0 %copy-start.35 = (f32[6,768]{1,0:T(8,128)S(1)}, f32[6,768]{1,0:T(8,128)}, u32[]{:S(2)}) copy-start(f32[6,768]{1,0:T(8,128)} %copy-done.34) | copy-start | bytes 55300 | tf_op jit(solution)/shard_map/while
  2770.1 398.9 %copy-start.40 = (f32[2,2,6,512,1]{3,2,1,4,0:T(8,128)S(1)}, f32[2,2,6,512,1]{3,2,1,4,0:T(8,128)}, u32[]{:S(2)}) copy-start(f32[2,2,6,512,1]{3,2,1,4,0:T(8,128)} %copy-done.39) | copy-start | bytes 147460 | tf_op jit(solution)/shard_map/while
  (90 other events, 392.3 us)
Sparse Core Ops, SparseCore 0:
  40.0 231.9 all-reduce.20
  429.8 19.4 all-reduce.22
  524.8 19.4 all-reduce.24
  575.7 230.4 all-reduce.20
  963.9 19.4 all-reduce.22
  1058.8 19.4 all-reduce.24
  1146.4 227.0 all-reduce.26
  1531.7 19.4 all-reduce.28
  1663.2 19.4 all-reduce.32
  1745.9 396.3 all-reduce.30
  2167.8 228.4 all-reduce.26
  2554.3 19.4 all-reduce.28
  2686.0 19.4 all-reduce.32
  2768.7 396.4 all-reduce.30
where the time goes:
time: 3320 us; the launch traced here: 3310 us
  waiting for transfers between devices  1640 us (49%)
  local copies, waits for them, and re-layouts  1090 us (33%)
  matrix products  253 us (8%)
  other arithmetic  169 us (5%)
  blocking collectives  115 us (3%)
    while x20, waiting for transfers between devices  1600 us
    slice x12, local copies, waits for them, and re-layouts, unpack(): packed[offset:offset + height * extent].reshape(height, extent)  403 us
    while x242, local copies, waits for them, and re-layouts  374 us
    broadcast_in_dim x2, local copies, waits for them, and re-layouts, backward_step(): jnp.concatenate([w_qkv_grad.reshape(-1), w_attn_grad.reshape(-1), w_in_gr...  108 us
    psum x1, blocking collectives, per_device(): shared_total = lax.psum(shared_acc, 'dp')  75.8 us
    reshape x16, local copies, waits for them, and re-layouts, unpack(): packed[offset:offset + height * extent].reshape(height, extent)  70.3 us
  transfers between devices with their start and end apart: 16, of which 10 were waited for; matrix products, arithmetic and copies ran while one was open for 17% of the time, Pallas kernels for 0%

commit v1 on v0

--- a/solution.py
+++ b/solution.py
@@ -316,7 +316,11 @@
     flat_grad = flat_acc
     flat_grad = flat_grad / LOSS_SCALE
     local_squares = jnp.sum(flat_grad * flat_grad)
-    shared_total = lax.psum(shared_acc, "dp")
+    shared_total = shared_acc
+    for hop in (1, 2, 4, 8):
+        shared_total = shared_total + lax.ppermute(
+            shared_total, "dp", [(dev, dev ^ hop) for dev in range(16)]
+        )
     total_squares = lax.psum(local_squares, ("dp", "mp"))
     shared_grad = shared_total / LOSS_SCALE
     norm_value = jnp.sqrt(total_squares + jnp.sum(shared_grad * shared_grad))

time: 3320 us -> 3260 us (0.982)
  blocking collectives: 115 us -> 39.6 us
    psum x1 -> x0, blocking collectives: 75.8 us -> none  [per_device(): shared_total = lax.psum(shared_acc, 'dp')]
  transfers between devices with their start and end apart: 16 -> 20, of which waited for: 10 -> 13; matrix products, arithmetic and copies ran while one was open for 17% -> 17% of each run, Pallas kernels for 0% -> 0%
where the time goes in v1:
time: 3260 us; the launch traced here: 3250 us
  waiting for transfers between devices  1650 us (51%)
  local copies, waits for them, and re-layouts  1090 us (33%)
  matrix products  253 us (8%)
  other arithmetic  170 us (5%)
  blocking collectives  39.6 us (1%)
    while x20, waiting for transfers between devices  1600 us
    slice x12, local copies, waits for them, and re-layouts, unpack(): packed[offset:offset + height * extent].reshape(height, extent)  403 us
    while x242, local copies, waits for them, and re-layouts  374 us
    broadcast_in_dim x2, local copies, waits for them, and re-layouts, backward_step(): jnp.concatenate([w_qkv_grad.reshape(-1), w_attn_grad.reshape(-1), w_in_gr...  108 us
    reshape x16, local copies, waits for them, and re-layouts, unpack(): packed[offset:offset + height * extent].reshape(height, extent)  70.3 us
  transfers between devices with their start and end apart: 20, of which 13 were waited for; matrix products, arithmetic and copies ran while one was open for 17% of the time, Pallas kernels for 0%

profile of v1, /device:TPU:0, one launch (start us, length us, event | category | flops | bytes accessed | tf_op | source)
XLA Modules:
  0.0 3249.2 jit_solution(8424791393531339129)
XLA Ops:
  18.3 1072.0 %while.46 = (s32[]{:T(128)}, bf16[2,2,512,768]{3,2,1,0:T(8,128)(2,1)}, bf16[2,2,32,768]{3,2,1,0:T(8,128)(2,1)S(1)}, bf16[2,2,512,6,64]{2,1,4,3,0:T(2,128)(2,1)},...) while((s32[]{:T(128)}, ...), condition=%wide.region_10.11_spmd.clone, body=%wide.region_0.10_spmd.clone.sunk | while | flops 8542994944 | bytes 398459968 | solution.py:179
  43.5 228.5 %all-reduce.21.cloned.1.call-done = bf16[3541248]{0:T(1024)(128)(2,1)} async-done(((bf16[3541248]{0:T(1024)(128)(2,1)}), bf16[3541248]{0:T(1024)(128)(2,1)}) %all-reduce.21.cloned.1.call-update) | async-done | bytes 7082512 | tf_op jit(solution)/shard_map/while
  272.0 69.0 %reshape.574 = bf16[1,3541248]{1,0:T(2,128)(2,1)S(1)} reshape(bf16[3541248]{0:T(1024)(128)(2,1)} %all-reduce.21.cloned.1.call-done) | data formatting | bytes 14164992 | tf_op jit(solution)/shard_map/while
  351.7 35.6 %slice_reduce_fusion.27 = bf16[884736]{0:T(1024)(128)(2,1)} fusion(bf16[1,3541248]{1,0:T(2,128)(2,1)S(1)} %reshape.574), kind=kLoop, calls=%fused_computation.30.clone.1 | loop fusion | bytes 3538944 | tf_op jit(solution)/shard_map/while/body/eval_jaxpr/slice | solution.py:43
  429.7 53.2 %slice_reduce_fusion.26 = (bf16[1179648]{0:T(1024)(128)(2,1)}, bf16[1179648]{0:T(1024)(128)(2,1)}) fusion(bf16[1,3541248]{1,0:T(2,128)(2,1)} %copy-done.2), kind=kLoop, calls=%fused_computation.28.clone.1 | loop fusion | bytes 9437184 | tf_op jit(solution)/shard_map/while/body/eval_jaxpr/slice | solution.py:43
  503.0 17.9 bitcast_dynamic-update-slice_fusion.12
  579.2 227.0 %all-reduce.21.cloned.1.call-done = bf16[3541248]{0:T(1024)(128)(2,1)} async-done(((bf16[3541248]{0:T(1024)(128)(2,1)}), bf16[3541248]{0:T(1024)(128)(2,1)}) %all-reduce.21.cloned.1.call-update) | async-done | bytes 7082512 | tf_op jit(solution)/shard_map/while
  806.2 68.9 %reshape.574 = bf16[1,3541248]{1,0:T(2,128)(2,1)S(1)} reshape(bf16[3541248]{0:T(1024)(128)(2,1)} %all-reduce.21.cloned.1.call-done) | data formatting | bytes 14164992 | tf_op jit(solution)/shard_map/while
  885.8 35.6 %slice_reduce_fusion.27 = bf16[884736]{0:T(1024)(128)(2,1)} fusion(bf16[1,3541248]{1,0:T(2,128)(2,1)S(1)} %reshape.574), kind=kLoop, calls=%fused_computation.30.clone.1 | loop fusion | bytes 3538944 | tf_op jit(solution)/shard_map/while/body/eval_jaxpr/slice | solution.py:43
  963.8 53.2 %slice_reduce_fusion.26 = (bf16[1179648]{0:T(1024)(128)(2,1)}, bf16[1179648]{0:T(1024)(128)(2,1)}) fusion(bf16[1,3541248]{1,0:T(2,128)(2,1)} %copy-done.2), kind=kLoop, calls=%fused_computation.28.clone.1 | loop fusion | bytes 9437184 | tf_op jit(solution)/shard_map/while/body/eval_jaxpr/slice | solution.py:43
  1037.1 17.9 bitcast_dynamic-update-slice_fusion.12
  1067.0 11.3 all-reduce.25.cloned.1.call-done
  1124.7 2047.9 %while.47 = (s32[]{:T(128)}, f32[6,768]{1,0:T(8,128)}, f32[1,221328]{1,0:T(1,128)}, f32[2,1024,768]{2,1,0:T(8,128)}, f32[2,1024,768]{2,1,0:T(8,128)}, /*index=5*...) while((s32[]{:T(128)}, f32[6,768]{1,0:T(8,128)}, ...), condition=%wide.region_36.37_spmd.clone, body=%wide.region_14.36_spmd.clone.sunk | while | flops 17043947520 | bytes 761370240 | solution.py:311
  1192.4 181.1 %all-reduce.27.cloned.1.call-done = bf16[3541248]{0:T(1024)(128)(2,1)} async-done(((bf16[3541248]{0:T(1024)(128)(2,1)}), bf16[3541248]{0:T(1024)(128)(2,1)}) %all-reduce.27.cloned.1.call-update) | async-done | bytes 7082512 | tf_op jit(solution)/shard_map/while
  1373.5 68.6 %reshape.582 = bf16[1,3541248]{1,0:T(2,128)(2,1)} reshape(bf16[3541248]{0:T(1024)(128)(2,1)} %all-reduce.27.cloned.1.call-done) | data formatting | bytes 14164992 | tf_op jit(solution)/shard_map/while
  1442.1 53.6 %slice_reduce_fusion.30 = (bf16[1179648]{0:T(1024)(128)(2,1)}, bf16[1179648]{0:T(1024)(128)(2,1)}) fusion(bf16[1,3541248]{1,0:T(2,128)(2,1)} %reshape.582), kind=kLoop, calls=%fused_computation.138.clone.1 | loop fusion | bytes 9437184 | tf_op jit(solution)/shard_map/while/body/eval_jaxpr/slice | solution.py:43
  1506.5 19.5 convert_reduce_fusion.15
  1531.6 11.8 slice_reduce_fusion.31
  1545.7 36.6 %slice_reduce_fusion.32 = bf16[884736]{0:T(1024)(128)(2,1)} fusion(bf16[1,3541248]{1,0:T(2,128)(2,1)} %reshape.582), kind=kLoop, calls=%fused_computation.141.clone.1 | loop fusion | bytes 3538944 | tf_op jit(solution)/shard_map/while/body/eval_jaxpr/slice | solution.py:43
  1626.0 11.4 multiply_reduce_fusion.27
  1691.5 54.1 %broadcast_in_dim.266 = f32[1,3541248]{1,0:T(1,128)} reshape(f32[3541248]{0:T(1024)} %constant_dynamic-update-slice_fusion.42) | data formatting | bytes 28329984 | tf_op jit(solution)/shard_map/while/body/eval_jaxpr/broadcast_in_dim | solution.py:286
  1750.8 391.5 %all-reduce.31.cloned.1.call-done = f32[1,3541248]{1,0:T(1,128)} async-done(((f32[1,3541248]{1,0:T(1,128)}), f32[1,3541248]{1,0:T(1,128)}) %all-reduce.31.cloned.1.call-update) | async-done | bytes 14165008 | tf_op jit(solution)/shard_map/while
  2213.9 182.4 %all-reduce.27.cloned.1.call-done = bf16[3541248]{0:T(1024)(128)(2,1)} async-done(((bf16[3541248]{0:T(1024)(128)(2,1)}), bf16[3541248]{0:T(1024)(128)(2,1)}) %all-reduce.27.cloned.1.call-update) | async-done | bytes 7082512 | tf_op jit(solution)/shard_map/while
  2396.3 68.6 %reshape.582 = bf16[1,3541248]{1,0:T(2,128)(2,1)} reshape(bf16[3541248]{0:T(1024)(128)(2,1)} %all-reduce.27.cloned.1.call-done) | data formatting | bytes 14164992 | tf_op jit(solution)/shard_map/while
  2464.9 53.3 %slice_reduce_fusion.30 = (bf16[1179648]{0:T(1024)(128)(2,1)}, bf16[1179648]{0:T(1024)(128)(2,1)}) fusion(bf16[1,3541248]{1,0:T(2,128)(2,1)} %reshape.582), kind=kLoop, calls=%fused_computation.138.clone.1 | loop fusion | bytes 9437184 | tf_op jit(solution)/shard_map/while/body/eval_jaxpr/slice | solution.py:43
  2529.1 19.6 convert_reduce_fusion.15
  2554.1 11.9 slice_reduce_fusion.31
  2568.3 36.6 %slice_reduce_fusion.32 = bf16[884736]{0:T(1024)(128)(2,1)} fusion(bf16[1,3541248]{1,0:T(2,128)(2,1)} %reshape.582), kind=kLoop, calls=%fused_computation.141.clone.1 | loop fusion | bytes 3538944 | tf_op jit(solution)/shard_map/while/body/eval_jaxpr/slice | solution.py:43
  2648.8 11.4 multiply_reduce_fusion.27
  2714.4 54.1 %broadcast_in_dim.266 = f32[1,3541248]{1,0:T(1,128)} reshape(f32[3541248]{0:T(1024)} %constant_dynamic-update-slice_fusion.42) | data formatting | bytes 28329984 | tf_op jit(solution)/shard_map/while/body/eval_jaxpr/broadcast_in_dim | solution.py:286
  2773.6 391.5 %all-reduce.31.cloned.1.call-done = f32[1,3541248]{1,0:T(1,128)} async-done(((f32[1,3541248]{1,0:T(1,128)}), f32[1,3541248]{1,0:T(1,128)}) %all-reduce.31.cloned.1.call-update) | async-done | bytes 14165008 | tf_op jit(solution)/shard_map/while
  3190.1 39.6 %psum.35 = f32[]{:T(128)} all-reduce(f32[]{:T(128)} %multiply_reduce_fusion.9), channel_id=1, replica_groups=mesh['dp'=16,'mp'=2] {'dp','mp'}, use_global_device_ids=true, to_apply=%region_38.39 | all-reduce | flops 1 | bytes 8 | tf_op jit(solution)/shard_map/psum | solution.py:324
  (575 shorter events, 704.3 us)
Async XLA Ops:
  18.3 1072.0 %copy-start.45 = (s32[128]{0:T(128)S(1)}, s32[128]{0:T(128)}, u32[]{:S(2)}) copy-start(s32[128]{0:T(128)} %add_bitcast_fusion.1) | copy-start | bytes 1540
  18.3 1079.7 %copy-start.50 = (s32[128,2]{0,1:T(2,128)S(1)}, s32[128,2]{0,1:T(2,128)}, u32[]{:S(2)}) copy-start(s32[128,2]{0,1:T(2,128)} %param.18) | copy-start | bytes 3076
  18.3 1089.5 %copy-start.46 = (s32[64]{0:T(128)S(1)}, s32[64]{0:T(128)}, u32[]{:S(2)}) copy-start(s32[64]{0:T(128)} %param.19) | copy-start | bytes 772
  18.5 253.5 %all-reduce.21.cloned.1.call-start = ((), (), s32[]{:S(2)}) async-start(), calls=%async_computation.2 | async-start | bytes 14168064 | tf_op jit(solution)/shard_map/while
  39.9 460.0 %all-reduce.23.cloned.1.call-start = ((), (), s32[]{:S(2)}) async-start(), calls=%async_computation.3 | async-start | bytes 3145728 | tf_op jit(solution)/shard_map/while/body/eval_jaxpr/psum | solution.py:149
  429.6 114.6 %all-reduce.25.cloned.1.call-start = ((), (), s32[]{:S(2)}) async-start(), calls=%async_computation.4 | async-start | bytes 3145728 | tf_op jit(solution)/shard_map/while/body/eval_jaxpr/psum | solution.py:157
  554.2 252.0 %all-reduce.21.cloned.1.call-start = ((), (), s32[]{:S(2)}) async-start(), calls=%async_computation.2 | async-start | bytes 14168064 | tf_op jit(solution)/shard_map/while
  575.6 458.4 %all-reduce.23.cloned.1.call-start = ((), (), s32[]{:S(2)}) async-start(), calls=%async_computation.3 | async-start | bytes 3145728 | tf_op jit(solution)/shard_map/while/body/eval_jaxpr/psum | solution.py:149
  963.7 114.6 %all-reduce.25.cloned.1.call-start = ((), (), s32[]{:S(2)}) async-start(), calls=%async_computation.4 | async-start | bytes 3145728 | tf_op jit(solution)/shard_map/while/body/eval_jaxpr/psum | solution.py:157
  1091.2 15.9 all-to-all-start
  1109.0 11.6 all-to-all-start.1
  1124.8 24.5 copy-start.34
  1124.8 51.6 %copy-start.39 = (f32[2,2,6,512,1]{3,2,1,4,0:T(8,128)}, f32[2,2,6,512,1]{3,2,1,4,0:T(8,128)S(1)}, u32[]{:S(2)}) copy-start(f32[2,2,6,512,1]{3,2,1,4,0:T(8,128)S(1)} %get-tuple-element.977) | copy-start | bytes 147460 | tf_op jit(solution)/shard_map/while
  1124.9 248.6 %all-reduce.27.cloned.1.call-start = ((), (), s32[]{:S(2)}) async-start(), calls=%async_computation.5 | async-start | bytes 14168064 | tf_op jit(solution)/shard_map/while
  1146.2 454.3 %all-reduce.29.cloned.1.call-start = ((), (), s32[]{:S(2)}) async-start(), calls=%async_computation.6 | async-start | bytes 3145728 | tf_op jit(solution)/shard_map/while/body/eval_jaxpr/psum | solution.py:242
  1531.5 215.7 %all-reduce.33.cloned.1.call-start = ((), (), s32[]{:S(2)}) async-start(), calls=%async_computation.8 | async-start | bytes 3145728 | tf_op jit(solution)/shard_map/while/body/eval_jaxpr/psum | solution.py:282
  1663.0 479.2 %all-reduce.31.cloned.1.call-start = ((), (), s32[]{:S(2)}) async-start(), calls=%async_computation.7 | async-start | bytes 28329984 | tf_op jit(solution)/shard_map/while
  1747.2 398.8 %copy-start.35 = (f32[6,768]{1,0:T(8,128)S(1)}, f32[6,768]{1,0:T(8,128)}, u32[]{:S(2)}) copy-start(f32[6,768]{1,0:T(8,128)} %copy-done.34) | copy-start | bytes 55300 | tf_op jit(solution)/shard_map/while
  1747.2 398.8 %copy-start.40 = (f32[2,2,6,512,1]{3,2,1,4,0:T(8,128)S(1)}, f32[2,2,6,512,1]{3,2,1,4,0:T(8,128)}, u32[]{:S(2)}) copy-start(f32[2,2,6,512,1]{3,2,1,4,0:T(8,128)} %copy-done.39) | copy-start | bytes 147460 | tf_op jit(solution)/shard_map/while
  2146.2 24.5 copy-start.34
  2146.2 51.8 %copy-start.39 = (f32[2,2,6,512,1]{3,2,1,4,0:T(8,128)}, f32[2,2,6,512,1]{3,2,1,4,0:T(8,128)S(1)}, u32[]{:S(2)}) copy-start(f32[2,2,6,512,1]{3,2,1,4,0:T(8,128)S(1)} %get-tuple-element.977) | copy-start | bytes 147460 | tf_op jit(solution)/shard_map/while
  2146.2 250.0 %all-reduce.27.cloned.1.call-start = ((), (), s32[]{:S(2)}) async-start(), calls=%async_computation.5 | async-start | bytes 14168064 | tf_op jit(solution)/shard_map/while
  2167.6 455.8 %all-reduce.29.cloned.1.call-start = ((), (), s32[]{:S(2)}) async-start(), calls=%async_computation.6 | async-start | bytes 3145728 | tf_op jit(solution)/shard_map/while/body/eval_jaxpr/psum | solution.py:242
  2529.1 21.2 copy-start.24
  2554.1 215.9 %all-reduce.33.cloned.1.call-start = ((), (), s32[]{:S(2)}) async-start(), calls=%async_computation.8 | async-start | bytes 3145728 | tf_op jit(solution)/shard_map/while/body/eval_jaxpr/psum | solution.py:282
  2685.8 479.3 %all-reduce.31.cloned.1.call-start = ((), (), s32[]{:S(2)}) async-start(), calls=%async_computation.7 | async-start | bytes 28329984 | tf_op jit(solution)/shard_map/while
  2770.0 399.0 %copy-start.35 = (f32[6,768]{1,0:T(8,128)S(1)}, f32[6,768]{1,0:T(8,128)}, u32[]{:S(2)}) copy-start(f32[6,768]{1,0:T(8,128)} %copy-done.34) | copy-start | bytes 55300 | tf_op jit(solution)/shard_map/while
  2770.0 398.9 %copy-start.40 = (f32[2,2,6,512,1]{3,2,1,4,0:T(8,128)S(1)}, f32[2,2,6,512,1]{3,2,1,4,0:T(8,128)}, u32[]{:S(2)}) copy-start(f32[2,2,6,512,1]{3,2,1,4,0:T(8,128)} %copy-done.39) | copy-start | bytes 147460 | tf_op jit(solution)/shard_map/while
  3172.6 4.1 collective-permute-start
  3177.5 3.8 collective-permute-start.1
  3181.3 4.1 collective-permute-start.2
  3185.4 44.4 %collective-permute-start.3 = (f32[6,768]{1,0:T(8,128)S(1)}, f32[6,768]{1,0:T(8,128)S(1)}, u32[]{:S(2)}, u32[]{:S(2)}) collective-permute-start(f32[6,768]{1,0:T(8,128)S(1)} %add.258), channel_id=1, source_target_pairs={{0,16},{2,18},{4,20},{6,22},{8,24},{10,26},{12,28},{14,30},{16,0},... | collective-permute-start | bytes 55304 | tf_op jit(solution)/shard_map/ppermute | solution.py:321
  (94 other events, 449.1 us)
Sparse Core Ops, SparseCore 0:
  40.0 231.9 all-reduce.20
  429.8 19.4 all-reduce.22
  524.8 19.4 all-reduce.24
  575.7 230.4 all-reduce.20
  963.9 19.4 all-reduce.22
  1058.8 19.4 all-reduce.24
  1146.4 227.0 all-reduce.26
  1531.6 19.4 all-reduce.28
  1663.1 19.4 all-reduce.32
  1745.8 396.3 all-reduce.30
  2167.7 228.4 all-reduce.26
  2554.2 19.4 all-reduce.28
  2685.9 19.4 all-reduce.32
  2768.6 396.3 all-reduce.30
